TPU v7x, 128 devices: a whole 4x4x4 slice. The times are simulated.
128 devices in a mesh: pr: 16 (over z, x), pc: 8 (over y, core).
Axes of the slice: x: 4, y: 4, z: 4, core: 2. Of those that a mesh axis runs over, the one named last changes fastest.
Arguments:
- trailing: float32 [20480, 20480], P('pr', 'pc'), may hold values from -25 to 25, as said below
- v_panels: float32 [6, 32, 20480], P(None, None, ('pr', 'pc')), may hold values from -0.078125 to 0.078125
- t_panels: float32 [6, 32, 32], replicated, may hold values from -0.2 to 0.5, as said below
Outputs:
- updated: float32 [20480, 20480], P('pr', 'pc')
- w_panels: float32 [6, 32, 20480], P(None, None, ('pr', 'pc'))
Inputs may be any that keep to these rules, and one draw needn't show every extreme that they name: trailing is exactly symmetric. `t_panels`: each panel's factor is upper triangular with diagonal entries of 0.25 to 0.5.
All inputs are finite; a program needn't handle non-finite values.
Results may differ from a plain program's by a relative error of at most 0.00013.
Values sent between devices are 32-bit elements; how exact they have to be, the bound alone decides.
A program may use at most 128 MiB of HBM per device.

v0:
```python
import jax
import jax.numpy as jnp
from jax import lax
from jax.sharding import PartitionSpec as P

HIGHEST = lax.Precision.HIGHEST


def contract(left_side, right_side, left_dim, right_dim, precision=HIGHEST):
    return lax.dot_general(
        left_side,
        right_side,
        (((left_dim,), (right_dim,)), ((), ())),
        precision=precision,
        preferred_element_type=jnp.float32,
    )


def small_coefficients(gram_y, gram_v, t_panels):
    panels, width, _ = t_panels.shape
    size = panels * width
    eye = jnp.eye(size, dtype=jnp.float32)
    zero = jnp.zeros((size, size), jnp.float32)
    of_y = jnp.concatenate([gram_y, zero, eye], axis=1)
    of_v = jnp.concatenate([gram_v, eye, zero], axis=1)
    of_w = []
    for panel in range(panels):
        here = slice(panel * width, (panel + 1) * width)
        of_x = of_y[here]
        if panel:
            done = jnp.concatenate(of_w, axis=0)
            before = slice(0, panel * width)
            left = jnp.concatenate([done[:, here], gram_v[before, here]], axis=0)
            right = jnp.concatenate([of_v[before], done], axis=0)
            of_x = of_x - contract(left, right, 0, 0)
        factor = t_panels[panel]
        scaled = contract(factor, of_x, 0, 0)
        middle = contract(scaled[:, here], factor, 1, 0)
        of_w.append(scaled - 0.5 * contract(middle, of_v[here], 1, 0))
    return jnp.concatenate(of_w, axis=0)


def per_device(trailing, v_panels, t_panels):
    rows, cols = (lax.axis_size("pr"), lax.axis_size("pc"))
    ratio = rows // cols
    panels, width, share = v_panels.shape
    size = panels * width
    v_own = v_panels.reshape(size, share)
    moves = []
    for i in range(rows):
        for j in range(cols):
            moves.append((i * cols + j, (i % ratio * cols + j) * cols + i // ratio))

    def columns(own):
        return lax.all_gather(lax.ppermute(own, ("pr", "pc"), moves), "pr", axis=1, tiled=True)

    v_row = lax.all_gather(v_own, "pc", axis=1, tiled=True)
    v_col = columns(v_own)
    partial_y = contract(v_col, trailing, 1, 1, lax.Precision.HIGH)
    y_own = lax.psum_scatter(partial_y, "pc", scatter_dimension=1, tiled=True)
    y_row = lax.all_gather(y_own, "pc", axis=1, tiled=True)
    y_col = columns(y_own)
    grams = contract(v_own, jnp.concatenate([y_own, v_own], axis=0), 1, 1)
    grams = lax.psum(grams, ("pr", "pc"))
    coefs = small_coefficients(grams[:, :size], grams[:, size:], t_panels)
    of_v, of_y = (coefs[:, size : 2 * size], coefs[:, 2 * size :])
    w_own = contract(of_v, v_own, 1, 0) + contract(of_y, y_own, 1, 0)
    left_v = contract(of_v + of_v.T, v_row, 1, 0) + contract(of_y, y_row, 1, 0)
    left_y = contract(of_y, v_row, 0, 0)
    left = jnp.concatenate([left_v, left_y], axis=0)
    right = jnp.concatenate([v_col, y_col], axis=0)
    matrix = trailing - contract(left, right, 0, 0, lax.Precision.HIGH)
    return (matrix, w_own.reshape(panels, width, share))


def solution(mesh):
    return jax.shard_map(
        per_device,
        mesh=mesh,
        in_specs=(P("pr", "pc"), P(None, None, ("pr", "pc")), P()),
        out_specs=(P("pr", "pc"), P(None, None, ("pr", "pc"))),
        check_vma=False,
    )
```

profile of v0, /device:TPU:1, one launch (start us, length us, event | category | flops | bytes accessed | tf_op | source)
XLA Modules:
  0.0 353.8 jit_solution(15385846826090534265)
XLA Ops:
  8.2 4.5 %collective-permute-start = (f32[192,160]{0,1:T(8,128)S(1)}, f32[192,160]{0,1:T(8,128)S(1)}, u32[]{:S(2)}, u32[]{:S(2)}) collective-permute-start(f32[192,160]{0,1:T(8,128)S(1)} %copy.12), channel_id=1, source_target_pairs={{0,0},{1,8},{2,16},{3,24},{4,32},{5,40},{6,48},{7,56},{8,64},{9,72... | collective-permute-start | bytes 368648 | tf_op jit(solution)/shard_map/ppermute | solution.py:55
  12.8 4.5 %collective-permute-done = f32[192,160]{0,1:T(8,128)S(1)} collective-permute-done((f32[192,160]{0,1:T(8,128)S(1)}, f32[192,160]{0,1:T(8,128)S(1)}, u32[]{:S(2)}, u32[]{:S(2)}) %collective-permute-start) | collective-permute-done | bytes 122912 | tf_op jit(solution)/shard_map/ppermute | solution.py:55
  18.0 53.5 %all-gather.3.cloned.1.call-done = f32[192,2560]{0,1:T(8,128)} async-done(((f32[192,160]{0,1:T(8,128)}), f32[192,2560]{0,1:T(8,128)}) %all-gather.3.cloned.1.call-update) | async-done | bytes 1966096 | tf_op jit(solution)/shard_map/all_gather | solution.py:55
  71.5 9.9 %fusion.106 = f32[192,1280]{0,1:T(8,128)} fusion(f32[192,2560]{0,1:T(8,128)} %all-gather.3.cloned.1.call-done, f32[1280,2560]{1,0:T(8,128)} %param.3), kind=kOutput, calls=%fused_computation.158 | convolution fusion | flops 3774873600 | bytes 16056320 | tf_op jit(solution)/shard_map/dot_general | solution.py:10
  82.2 15.8 %all_gather.13 = f32[192,1280]{0,1:T(8,128)S(1)} all-gather(f32[192,160]{0,1:T(8,128)S(1)} %copy.12), channel_id=1, replica_groups=mesh['pr'=16,'pc'=8] {'pc'}, dimensions={1}, use_global_device_ids=true | all-gather | bytes 1105920 | tf_op jit(solution)/shard_map/all_gather | solution.py:57
  98.0 13.6 %reduce-scatter.2.cloned.1.call-done = f32[192,160]{0,1:T(8,128)} async-done(((f32[192,1280]{0,1:T(8,128)}), f32[192,160]{0,1:T(8,128)}) %reduce-scatter.2.cloned.1.call-update) | async-done | bytes 122896 | tf_op jit(solution)/shard_map/reduce_scatter | solution.py:60
  111.6 2.2 convolution_bitcast_fusion
  113.9 6.3 %collective-permute-start.1 = (f32[192,160]{0,1:T(8,128)}, f32[192,160]{0,1:T(8,128)S(1)}, u32[]{:S(2)}, u32[]{:S(2)}) collective-permute-start(f32[192,160]{0,1:T(8,128)} %reduce-scatter.2.cloned.1.call-done), channel_id=1, source_target_pairs={{0,0},{1,8},{2,16},{3,24},{4,32},{5,40},{6,48},{7,56},{8,64},{9,72... | collective-permute-start | bytes 368648 | tf_op jit(solution)/shard_map/ppermute | solution.py:55
  120.2 20.7 %all_gather.14 = f32[192,1280]{0,1:T(8,128)S(1)} all-gather(f32[192,160]{0,1:T(8,128)} %reduce-scatter.2.cloned.1.call-done), channel_id=1, replica_groups=mesh['pr'=16,'pc'=8] {'pc'}, dimensions={1}, use_global_device_ids=true | all-gather | bytes 1105920 | tf_op jit(solution)/shard_map/all_gather | solution.py:61
  141.6 118.4 %all-reduce.2.cloned.1.call-done = f32[192,384]{1,0:T(8,128)} async-done(((f32[192,384]{1,0:T(8,128)}), f32[192,384]{1,0:T(8,128)}) %all-reduce.2.cloned.1.call-update) | async-done | bytes 294928 | tf_op jit(solution)/shard_map/psum | solution.py:64
  260.0 1.1 fusion.105
  261.2 2.0 pad_maximum_fusion.1
  269.1 1.2 convolution_bitcast_fusion.6
  272.9 1.2 convolution_subtract_fusion.3
  277.9 1.3 convolution_subtract_fusion.5
  282.8 1.5 copy.16
  284.2 1.5 convolution_subtract_fusion.4
  287.4 1.5 fusion.60
  288.9 1.5 slice.195
  290.5 1.5 copy.19
  292.0 1.6 slice.201
  293.6 1.6 copy.21
  295.2 1.9 constant_dynamic-update-slice_fusion.5
  298.6 1.6 convolution_subtract_fusion.2
  304.6 1.8 convolution_subtract_fusion.1
  309.2 1.1 slice.205
  310.3 1.3 fusion.30
  311.5 1.6 convolution_add_fusion.1
  314.0 3.9 %fusion.32 = f32[192,1280]{1,0:T(8,128)} fusion(f32[192,1280]{0,1:T(8,128)S(1)} %all_gather.13, f32[192,576]{1,0:T(8,128)} %fusion.7), kind=kOutput, calls=%fused_computation.59 | convolution fusion | flops 566231040 | bytes 2162688 | tf_op jit(solution)/shard_map/dot_general | solution.py:10
  317.9 2.4 fusion.28
  320.4 3.4 convolution_add_fusion
  323.8 23.5 %convolution_subtract_fusion = f32[1280,2560]{1,0:T(8,128)} fusion(f32[1280,2560]{1,0:T(8,128)} %param.3, f32[192,2560]{0,1:T(8,128)} %all-gather.5.cloned.1.call-done, f32[192,2560]{0,1:T(8,128)} %all-gather.3.cloned.1.call-done, f32[192,1280]{1,0:T(8,128)S(1)} %copy-done, f32[192,1280]{1,0:T(8,128)} %convolution_add_fusion), kind=kOutput, calls=%fused_computation | convolution fusion | flops 7554498560 | bytes 32112640 | tf_op jit(solution)/shard_map/dot_general | solution.py:10
  (62 shorter events, 30.5 us)
Async XLA Ops:
  7.2 64.3 %all-gather.3.cloned.1.call-start = ((), (), s32[]{:S(2)}) async-start(), calls=%async_computation.1 | async-start | bytes 2785280 | tf_op jit(solution)/shard_map/all_gather | solution.py:55
  8.2 9.0 %collective-permute-start = (f32[192,160]{0,1:T(8,128)S(1)}, f32[192,160]{0,1:T(8,128)S(1)}, u32[]{:S(2)}, u32[]{:S(2)}) collective-permute-start(f32[192,160]{0,1:T(8,128)S(1)} %copy.12), channel_id=1, source_target_pairs={{0,0},{1,8},{2,16},{3,24},{4,32},{5,40},{6,48},{7,56},{8,64},{9,72... | collective-permute-start | bytes 368648 | tf_op jit(solution)/shard_map/ppermute | solution.py:55
  17.3 0.7 copy-start.5
  18.0 93.6 %reduce-scatter.2.cloned.1.call-start = ((), (), s32[]{:S(2)}) async-start(), calls=%async_computation.2 | async-start | bytes 1474560 | tf_op jit(solution)/shard_map/reduce_scatter | solution.py:60
  81.4 30.2 %copy-start.1 = (f32[6,32,160]{2,1,0:T(8,128)S(1)}, f32[6,32,160]{2,1,0:T(8,128)}, u32[]{:S(2)}) copy-start(f32[6,32,160]{2,1,0:T(8,128)} %param.4) | copy-start | bytes 368644
  81.5 178.6 %all-reduce.2.cloned.1.call-start = ((), (), s32[]{:S(2)}) async-start(), calls=%async_computation.3 | async-start | bytes 589824 | tf_op jit(solution)/shard_map/psum | solution.py:64
  113.8 210.0 %all-gather.5.cloned.1.call-start = ((), (), s32[]{:S(2)}) async-start(), calls=%async_computation.4 | async-start | bytes 2785280 | tf_op jit(solution)/shard_map/all_gather | solution.py:55
  113.9 27.0 %collective-permute-start.1 = (f32[192,160]{0,1:T(8,128)}, f32[192,160]{0,1:T(8,128)S(1)}, u32[]{:S(2)}, u32[]{:S(2)}) collective-permute-start(f32[192,160]{0,1:T(8,128)} %reduce-scatter.2.cloned.1.call-done), channel_id=1, source_target_pairs={{0,0},{1,8},{2,16},{3,24},{4,32},{5,40},{6,48},{7,56},{8,64},{9,72... | collective-permute-start | bytes 368648 | tf_op jit(solution)/shard_map/ppermute | solution.py:55
  140.9 0.7 copy-start.4
  277.0 0.8 copy-start.6
  286.8 0.6 copy-start.3
  297.7 12.6 %copy-start.2 = (f32[192,160]{0,1:T(8,128)S(1)}, f32[192,160]{0,1:T(8,128)}, u32[]{:S(2)}) copy-start(f32[192,160]{0,1:T(8,128)} %reduce-scatter.2.cloned.1.call-done) | copy-start | bytes 368644
  320.3 3.4 copy-start
Sparse Core Ops, SparseCore 0:
  18.1 53.3 all-gather.2
  81.6 29.9 reduce-scatter.1
  116.9 143.0 all-reduce.1
  262.0 44.4 all-gather.4
where the time goes:
time: 355 us; the launch traced here: 354 us
  waiting for transfers between devices  190 us (54%)
  matrix products  74.1 us (21%)
  blocking collectives  36.6 us (10%)
  local copies, waits for them, and re-layouts  24.1 us (7%)
  between operations  14 us (4%)
  starting transfers between devices  11 us (3%)
  other arithmetic  4.12 us (1%)
    psum x1, waiting for transfers between devices, per_device(): grams = lax.psum(grams, ('pr', 'pc'))  118 us
    dot_general x31, matrix products, contract(): lax.dot_general(left_side, right_side, (((left_dim,), (right_dim,)), ((),...  74.1 us
    all_gather x2, waiting for transfers between devices, columns(): lax.all_gather(lax.ppermute(own, ('pr', 'pc'), moves), 'pr', axis=1, tile...  53.5 us
    all_gather x1, blocking collectives, per_device(): y_row = lax.all_gather(y_own, 'pc', axis=1, tiled=True)  20.7 us
    all_gather x1, blocking collectives, per_device(): v_row = lax.all_gather(v_own, 'pc', axis=1, tiled=True)  15.8 us
    slice x15, local copies, waits for them, and re-layouts, small_coefficients(): left = jnp.concatenate([done[:, here], gram_v[before, here]], axis=0)  14.3 us
    reduce_scatter x1, waiting for transfers between devices, per_device(): y_own = lax.psum_scatter(partial_y, 'pc', scatter_dimension=1, tiled=True)  13.6 us
    ppermute x2, starting transfers between devices, columns(): lax.ppermute(own, ('pr', 'pc'), moves)  10.8 us
  transfers between devices with their start and end apart: 6, of which 4 were waited for; matrix products, arithmetic and copies ran while one was open for 18% of the time, Pallas kernels for 0%

commit v1 on v0

--- a/solution.py
+++ b/solution.py
@@ -54,7 +54,22 @@
     def columns(own):
         return lax.all_gather(lax.ppermute(own, ("pr", "pc"), moves), "pr", axis=1, tiled=True)
 
-    v_row = lax.all_gather(v_own, "pc", axis=1, tiled=True)
+    ways, here_2, step = (lax.axis_size("pc"), lax.axis_index("pc"), v_own.shape[1])
+    shape = [n * ways if d == 1 else n for d, n in enumerate(v_own.shape)]
+    v_row = lax.dynamic_update_slice_in_dim(
+        jnp.zeros(shape, v_own.dtype), v_own, here_2 * step, axis=1
+    )
+    going_up = going_down = v_own
+    for far in range(1, ways // 2 + 1):
+        going_up = lax.ppermute(going_up, "pc", [(d, (d + 1) % ways) for d in range(ways)])
+        v_row = lax.dynamic_update_slice_in_dim(
+            v_row, going_up, (here_2 - far) % ways * step, axis=1
+        )
+        if 2 * far < ways:
+            going_down = lax.ppermute(going_down, "pc", [(d, (d - 1) % ways) for d in range(ways)])
+            v_row = lax.dynamic_update_slice_in_dim(
+                v_row, going_down, (here_2 + far) % ways * step, axis=1
+            )
     v_col = columns(v_own)
     partial_y = contract(v_col, trailing, 1, 1, lax.Precision.HIGH)
     y_own = lax.psum_scatter(partial_y, "pc", scatter_dimension=1, tiled=True)

time: 355 us -> 338 us (0.952)
  blocking collectives: 36.6 us -> 22 us
  matrix products: 74.1 us -> 59.5 us
  starting transfers between devices: 11 us -> 21.3 us
  waiting for transfers between devices: 190 us -> 197 us
  other arithmetic: 4.12 us -> 0.39 us
    all_gather x1 -> x0, blocking collectives: 15.8 us -> none  [per_device(): v_row = lax.all_gather(v_own, 'pc', axis=1, tiled=True)]
    dot_general x31, matrix products: 74.1 us -> 59.5 us  [contract(): lax.dot_general(left_side, right_side, (((left_dim,), (right_dim,)), ((),...]
    all_gather x2, waiting for transfers between devices: 53.5 us -> 67.6 us  [columns(): lax.all_gather(lax.ppermute(own, ('pr', 'pc'), moves), 'pr', axis=1, tile...]
    reduce_scatter x1, waiting for transfers between devices: 13.6 us -> 0.02 us  [per_device(): y_own = lax.psum_scatter(partial_y, 'pc', scatter_dimension=1, tiled=True)]
    dynamic_update_slice x0 -> x8, local copies, waits for them, and re-layouts: none -> 13 us  [the longest x4 6.01 us: per_device(): lax.dynamic_update_slice_in_dim(v_row, going_up, (here_2 - far) % ways *...]
    slice x15, local copies, waits for them, and re-layouts: 14.3 us -> 1.89 us  [small_coefficients(): left = jnp.concatenate([done[:, here], gram_v[before, here]], axis=0)]
    ppermute x0 -> x7, starting transfers between devices: none -> 10.5 us  [the longest x4 9.52 us: per_device(): lax.ppermute(going_up, 'pc', [(d, (d + 1) % ways) for d in range(ways)])]
    ppermute x0 -> x7, waiting for transfers between devices: none -> 8.65 us  [the longest x4 7.63 us: per_device(): lax.ppermute(going_up, 'pc', [(d, (d + 1) % ways) for d in range(ways)])]
  transfers between devices with their start and end apart: 6 -> 13, of which waited for: 4 -> 8; matrix products, arithmetic and copies ran while one was open for 18% -> 13% of each run, Pallas kernels for 0% -> 0%
where the time goes in v1:
time: 338 us; the launch traced here: 337 us
  waiting for transfers between devices  197 us (58%)
  matrix products  59.5 us (18%)
  local copies, waits for them, and re-layouts  23.2 us (7%)
  blocking collectives  22 us (7%)
  starting transfers between devices  21.3 us (6%)
  between operations  14.1 us (4%)
    psum x1, waiting for transfers between devices, per_device(): grams = lax.psum(grams, ('pr', 'pc'))  116 us
    all_gather x2, waiting for transfers between devices, columns(): lax.all_gather(lax.ppermute(own, ('pr', 'pc'), moves), 'pr', axis=1, tile...  67.6 us
    dot_general x31, matrix products, contract(): lax.dot_general(left_side, right_side, (((left_dim,), (right_dim,)), ((),...  59.5 us
    all_gather x1, blocking collectives, per_device(): y_row = lax.all_gather(y_own, 'pc', axis=1, tiled=True)  22 us
    ppermute x2, starting transfers between devices, columns(): lax.ppermute(own, ('pr', 'pc'), moves)  10.6 us
    ppermute x4, starting transfers between devices, per_device(): lax.ppermute(going_up, 'pc', [(d, (d + 1) % ways) for d in range(ways)])  9.52 us
    ppermute x4, waiting for transfers between devices, per_device(): lax.ppermute(going_up, 'pc', [(d, (d + 1) % ways) for d in range(ways)])  7.63 us
  transfers between devices with their start and end apart: 13, of which 8 were waited for; matrix products, arithmetic and copies ran while one was open for 13% of the time, Pallas kernels for 0%

profile of v1, /device:TPU:1, one launch (start us, length us, event | category | flops | bytes accessed | tf_op | source)
XLA Modules:
  0.0 337.3 jit_solution(7235087431585711557)
XLA Ops:
  8.2 4.5 %collective-permute-start = (f32[192,160]{0,1:T(8,128)S(1)}, f32[192,160]{0,1:T(8,128)S(1)}, u32[]{:S(2)}, u32[]{:S(2)}) collective-permute-start(f32[192,160]{0,1:T(8,128)S(1)} %copy.12), channel_id=1, source_target_pairs={{0,0},{1,8},{2,16},{3,24},{4,32},{5,40},{6,48},{7,56},{8,64},{9,72... | collective-permute-start | bytes 368648 | tf_op jit(solution)/shard_map/ppermute | solution.py:55
  12.8 4.5 %collective-permute-done = f32[192,160]{0,1:T(8,128)S(1)} collective-permute-done((f32[192,160]{0,1:T(8,128)S(1)}, f32[192,160]{0,1:T(8,128)S(1)}, u32[]{:S(2)}, u32[]{:S(2)}) %collective-permute-start) | collective-permute-done | bytes 122912 | tf_op jit(solution)/shard_map/ppermute | solution.py:55
  18.0 53.5 %all-gather.3.cloned.1.call-done = f32[192,2560]{0,1:T(8,128)} async-done(((f32[192,160]{0,1:T(8,128)}), f32[192,2560]{0,1:T(8,128)}) %all-gather.3.cloned.1.call-update) | async-done | bytes 1966096 | tf_op jit(solution)/shard_map/all_gather | solution.py:55
  71.5 9.9 %fusion.106 = f32[192,1280]{0,1:T(8,128)} fusion(f32[192,2560]{0,1:T(8,128)} %all-gather.3.cloned.1.call-done, f32[1280,2560]{1,0:T(8,128)} %param.3), kind=kOutput, calls=%fused_computation.158 | convolution fusion | flops 3774873600 | bytes 16056320 | tf_op jit(solution)/shard_map/dot_general | solution.py:10
  81.5 2.1 collective-permute-start.1
  83.6 2.6 collective-permute-done.1
  86.2 2.5 collective-permute-start.3
  88.8 3.4 collective-permute-done.3
  92.2 2.5 collective-permute-start.5
  96.5 1.7 collective-permute-done.5
  98.2 2.5 collective-permute-start.7
  100.7 1.8 dynamic_update_slice.24
  102.6 1.5 dynamic_update_slice.25
  104.1 1.8 dynamic_update_slice.26
  107.1 1.8 dynamic_update_slice.28
  108.9 1.5 dynamic_update_slice.29
  110.4 1.5 dynamic_update_slice.30
  112.0 1.8 dynamic_update_slice.31
  113.8 2.4 convolution_bitcast_fusion
  116.3 6.1 %collective-permute-start.8 = (f32[192,160]{0,1:T(8,128)}, f32[192,160]{0,1:T(8,128)S(1)}, u32[]{:S(2)}, u32[]{:S(2)}) collective-permute-start(f32[192,160]{0,1:T(8,128)} %reduce-scatter.2.cloned.1.call-done), channel_id=1, source_target_pairs={{0,0},{1,8},{2,16},{3,24},{4,32},{5,40},{6,48},{7,56},{8,64},{9,72... | collective-permute-start | bytes 368648 | tf_op jit(solution)/shard_map/ppermute | solution.py:55
  122.4 22.0 %all_gather.10 = f32[192,1280]{0,1:T(8,128)} all-gather(f32[192,160]{0,1:T(8,128)} %reduce-scatter.2.cloned.1.call-done), channel_id=1, replica_groups=mesh['pr'=16,'pc'=8] {'pc'}, dimensions={1}, use_global_device_ids=true | all-gather | bytes 1105920 | tf_op jit(solution)/shard_map/all_gather | solution.py:76
  145.2 115.9 %all-reduce.2.cloned.1.call-done = f32[192,384]{1,0:T(8,128)} async-done(((f32[192,384]{1,0:T(8,128)}), f32[192,384]{1,0:T(8,128)}) %all-reduce.2.cloned.1.call-update) | async-done | bytes 294928 | tf_op jit(solution)/shard_map/psum | solution.py:79
  267.1 1.4 convolution_subtract_fusion.3
  270.8 1.3 convolution_subtract_fusion.5
  273.7 1.5 convolution_subtract_fusion.4
  277.0 1.6 convolution_subtract_fusion.2
  280.9 1.7 convolution_subtract_fusion.1
  285.4 2.1 fusion.31
  287.5 2.9 fusion.33
  290.4 3.2 convolution_add_fusion
  293.5 14.1 %all-gather.5.cloned.1.call-done = f32[192,2560]{0,1:T(8,128)} async-done(((f32[192,160]{0,1:T(8,128)}), f32[192,2560]{0,1:T(8,128)}) %all-gather.5.cloned.1.call-update) | async-done | bytes 1966096 | tf_op jit(solution)/shard_map/all_gather | solution.py:55
  307.7 23.1 %convolution_subtract_fusion = f32[1280,2560]{1,0:T(8,128)} fusion(f32[1280,2560]{1,0:T(8,128)} %param.3, f32[192,2560]{0,1:T(8,128)} %all-gather.5.cloned.1.call-done, f32[192,2560]{0,1:T(8,128)S(1)} %copy-done, f32[192,1280]{1,0:T(8,128)} %fusion.31, f32[192,1280]{1,0:T(8,128)} %convolution_add_fusion), kind=kOutput, calls=%fused_computation | convolution fusion | flops 7554498560 | bytes 32112640 | tf_op jit(solution)/shard_map/dot_general | solution.py:10
  (92 shorter events, 22.4 us)
Async XLA Ops:
  7.2 64.3 %all-gather.3.cloned.1.call-start = ((), (), s32[]{:S(2)}) async-start(), calls=%async_computation.1 | async-start | bytes 2785280 | tf_op jit(solution)/shard_map/all_gather | solution.py:55
  8.2 9.0 %collective-permute-start = (f32[192,160]{0,1:T(8,128)S(1)}, f32[192,160]{0,1:T(8,128)S(1)}, u32[]{:S(2)}, u32[]{:S(2)}) collective-permute-start(f32[192,160]{0,1:T(8,128)S(1)} %copy.12), channel_id=1, source_target_pairs={{0,0},{1,8},{2,16},{3,24},{4,32},{5,40},{6,48},{7,56},{8,64},{9,72... | collective-permute-start | bytes 368648 | tf_op jit(solution)/shard_map/ppermute | solution.py:55
  17.3 0.7 copy-start.9
  18.0 63.5 %copy-start.2 = (f32[6,32,160]{2,1,0:T(8,128)S(1)}, f32[6,32,160]{2,1,0:T(8,128)}, u32[]{:S(2)}) copy-start(f32[6,32,160]{2,1,0:T(8,128)} %param.4) | copy-start | bytes 368644
  18.0 95.8 %reduce-scatter.2.cloned.1.call-start = ((), (), s32[]{:S(2)}) async-start(), calls=%async_computation.2 | async-start | bytes 1474560 | tf_op jit(solution)/shard_map/reduce_scatter | solution.py:75
  81.5 179.6 %all-reduce.2.cloned.1.call-start = ((), (), s32[]{:S(2)}) async-start(), calls=%async_computation.3 | async-start | bytes 589824 | tf_op jit(solution)/shard_map/psum | solution.py:79
  81.5 4.7 %collective-permute-start.1 = (f32[192,160]{1,0:T(8,128)S(1)}, f32[192,160]{1,0:T(8,128)S(1)}, u32[]{:S(2)}, u32[]{:S(2)}) collective-permute-start(f32[192,160]{1,0:T(8,128)S(1)} %bitcast.71), channel_id=1, source_target_pairs={{0,1},{1,2},{2,3},{3,4},{4,5},{5,6},{6,7},{7,0},{8,9},{9,10},{10,1... | collective-permute-start | bytes 368648 | tf_op jit(solution)/shard_map/ppermute | solution.py:64
  83.6 5.1 %collective-permute-start.2 = (f32[192,160]{1,0:T(8,128)S(1)}, f32[192,160]{1,0:T(8,128)S(1)}, u32[]{:S(2)}, u32[]{:S(2)}) collective-permute-start(f32[192,160]{1,0:T(8,128)S(1)} %bitcast.72), channel_id=1, source_target_pairs={{0,7},{1,0},{2,1},{3,2},{4,3},{5,4},{6,5},{7,6},{8,15},{9,8},{10,9... | collective-permute-start | bytes 368648 | tf_op jit(solution)/shard_map/ppermute | solution.py:69
  86.2 6.0 %collective-permute-start.3 = (f32[192,160]{1,0:T(8,128)S(1)}, f32[192,160]{1,0:T(8,128)S(1)}, u32[]{:S(2)}, u32[]{:S(2)}) collective-permute-start(f32[192,160]{1,0:T(8,128)S(1)} %collective-permute-done.1), channel_id=1, source_target_pairs={{0,1},{1,2},{2,3},{3,4},{4,5},{5,6},{6,7},{7,0},{8,9},{9,10},{10,1... | collective-permute-start | bytes 368648 | tf_op jit(solution)/shard_map/ppermute | solution.py:64
  88.7 7.0 %collective-permute-start.4 = (f32[192,160]{1,0:T(8,128)S(1)}, f32[192,160]{1,0:T(8,128)S(1)}, u32[]{:S(2)}, u32[]{:S(2)}) collective-permute-start(f32[192,160]{1,0:T(8,128)S(1)} %collective-permute-done.2), channel_id=1, source_target_pairs={{0,7},{1,0},{2,1},{3,2},{4,3},{5,4},{6,5},{7,6},{8,15},{9,8},{10,9... | collective-permute-start | bytes 368648 | tf_op jit(solution)/shard_map/ppermute | solution.py:69
  92.2 6.0 %collective-permute-start.5 = (f32[192,160]{1,0:T(8,128)S(1)}, f32[192,160]{1,0:T(8,128)S(1)}, u32[]{:S(2)}, u32[]{:S(2)}) collective-permute-start(f32[192,160]{1,0:T(8,128)S(1)} %collective-permute-done.3), channel_id=1, source_target_pairs={{0,1},{1,2},{2,3},{3,4},{4,5},{5,6},{6,7},{7,0},{8,9},{9,10},{10,1... | collective-permute-start | bytes 368648 | tf_op jit(solution)/shard_map/ppermute | solution.py:64
  95.7 14.7 %collective-permute-start.6 = (f32[192,160]{1,0:T(8,128)S(1)}, f32[192,160]{1,0:T(8,128)S(1)}, u32[]{:S(2)}, u32[]{:S(2)}) collective-permute-start(f32[192,160]{1,0:T(8,128)S(1)} %collective-permute-done.4), channel_id=1, source_target_pairs={{0,7},{1,0},{2,1},{3,2},{4,3},{5,4},{6,5},{7,6},{8,15},{9,8},{10,9... | collective-permute-start | bytes 368648 | tf_op jit(solution)/shard_map/ppermute | solution.py:69
  98.2 13.8 %collective-permute-start.7 = (f32[192,160]{1,0:T(8,128)S(1)}, f32[192,160]{1,0:T(8,128)S(1)}, u32[]{:S(2)}, u32[]{:S(2)}) collective-permute-start(f32[192,160]{1,0:T(8,128)S(1)} %collective-permute-done.5), channel_id=1, source_target_pairs={{0,1},{1,2},{2,3},{3,4},{4,5},{5,6},{6,7},{7,0},{8,9},{9,10},{10,1... | collective-permute-start | bytes 368648 | tf_op jit(solution)/shard_map/ppermute | solution.py:64
  113.8 171.6 %copy-start.1 = (f32[192,1280]{1,0:T(8,128)}, f32[192,1280]{1,0:T(8,128)S(1)}, u32[]{:S(2)}) copy-start(f32[192,1280]{1,0:T(8,128)S(1)} %dynamic_update_slice.31) | copy-start | bytes 2949124
  116.2 191.4 %all-gather.5.cloned.1.call-start = ((), (), s32[]{:S(2)}) async-start(), calls=%async_computation.4 | async-start | bytes 2785280 | tf_op jit(solution)/shard_map/all_gather | solution.py:55
  116.3 28.2 %collective-permute-start.8 = (f32[192,160]{0,1:T(8,128)}, f32[192,160]{0,1:T(8,128)S(1)}, u32[]{:S(2)}, u32[]{:S(2)}) collective-permute-start(f32[192,160]{0,1:T(8,128)} %reduce-scatter.2.cloned.1.call-done), channel_id=1, source_target_pairs={{0,0},{1,8},{2,16},{3,24},{4,32},{5,40},{6,48},{7,56},{8,64},{9,72... | collective-permute-start | bytes 368648 | tf_op jit(solution)/shard_map/ppermute | solution.py:55
  144.5 0.7 copy-start.8
  145.2 120.5 %copy-start.7 = (f32[6,32,32]{2,1,0:T(8,128)S(1)}, f32[6,32,32]{2,1,0:T(8,128)}, u32[]{:S(2)}) copy-start(f32[6,32,32]{2,1,0:T(8,128)} %param.5) | copy-start | bytes 73732
  261.1 4.3 %copy-start.6 = (f32[192,384]{1,0:T(8,128)S(1)}, f32[192,384]{1,0:T(8,128)}, u32[]{:S(2)}) copy-start(f32[192,384]{1,0:T(8,128)} %all-reduce.2.cloned.1.call-done) | copy-start | bytes 884740
  262.5 3.4 %copy-start.4 = (f32[192,576]{1,0:T(8,128)}, f32[192,576]{1,0:T(8,128)S(1)}, u32[]{:S(2)}) copy-start(f32[192,576]{1,0:T(8,128)S(1)} %get-tuple-element.5) | copy-start | bytes 1327108
  267.0 2.0 copy-start.3
  269.9 0.8 copy-start.10
  275.7 7.8 %copy-start.5 = (f32[192,160]{0,1:T(8,128)S(1)}, f32[192,160]{0,1:T(8,128)}, u32[]{:S(2)}) copy-start(f32[192,160]{0,1:T(8,128)} %reduce-scatter.2.cloned.1.call-done) | copy-start | bytes 368644
  287.5 20.2 %copy-start = (f32[192,2560]{0,1:T(8,128)S(1)}, f32[192,2560]{0,1:T(8,128)}, u32[]{:S(2)}) copy-start(f32[192,2560]{0,1:T(8,128)} %all-gather.3.cloned.1.call-done) | copy-start | bytes 5898244
Sparse Core Ops, SparseCore 0:
  18.1 53.3 all-gather.2
  81.6 30.1 reduce-scatter.1
  117.1 143.9 all-reduce.1
  263.1 44.5 all-gather.4
